TPU v7x, 512 devices: a whole 4x4x16 slice. The times are simulated.
512 devices in a mesh: row: 32 (over x, z_lo, core), col: 16 (over y, z_hi).
Axes of the slice: x: 4, y: 4, z: 16 (z_hi: 4, z_lo: 4; z = z_hi * 4 + z_lo), core: 2. Of those that a mesh axis runs over, the one named last changes fastest.
Arguments:
- hidden_img: bfloat16 [16384, 2432], P('row', 'col'), may hold values from -75 to 75
- hidden_txt: bfloat16 [3072, 2432], P('row', 'col'), may hold values from -75 to 75
- text_len: int32 [16], replicated, may hold values from 1 to 154, as said below
- step_index: int32 [16], replicated, may hold values from 0 to 27
- latent: float32 [16384, 64], P('row'), may hold values from -6 to 6
- cond: float32 [16, 2432], P(None, 'row'), may hold values from -6 to 6
- mod_weight: bfloat16 [2432, 7, 2432], P('row', None, 'col'), may hold values from -0.125 to 0.125
- qkv_weight: bfloat16 [2432, 3, 2048], P('row', None, 'col'), may hold values from -0.125 to 0.125
- kv_text_weight: bfloat16 [2432, 2, 2048], P('row', None, 'col'), may hold values from -0.125 to 0.125
- q_gain: float32 [64], replicated, may hold values from 0.5 to 6
- k_gain: float32 [2, 64], replicated, may hold values from 0.5 to 6
- out_weight: bfloat16 [2048, 2432], P('row', 'col'), may hold values from -6 to 6
- final_weight: bfloat16 [2432, 64], P('row'), may hold values from -0.125 to 0.125
Outputs:
- velocity: float32 [16384, 64], P('row')
- latent_next: float32 [16384, 64], P('row')
Inputs may be any that keep to these rules, and one draw needn't show every extreme that they name: `text_len`: some request has exactly 154 text tokens in every draw.
All inputs are finite; a program needn't handle non-finite values.
Results may differ from a plain program's by a relative error of at most 0.015.
The roundings to bfloat16 on the way count: a program that leaves them out, or rounds other values in their place, can miss the bound.
Values may be sent and summed in bfloat16 or wider, within the bound.
A program may use at most 64 MiB of HBM per device.

v0:
```python
import jax
import jax.numpy as jnp
from jax import lax
from jax.sharding import PartitionSpec as P

STEPS = 28
EPS_NORM = 1e-06


def partner_2(block, axis, distance):
    count = lax.axis_size(axis)
    route = []
    for low in range(count):
        high = low | 1 << distance
        if high != low and high < count:
            route += [(low, high), (high, low)]
    return lax.ppermute(block, axis, route)


def modulate_full(values, offset, stretch):
    average = jnp.mean(values, axis=1, keepdims=True)
    mean_square = jnp.mean(values * values, axis=1, keepdims=True)
    normed = (values - average) * lax.rsqrt(mean_square - average * average + EPS_NORM)
    return (normed * (1.0 + stretch) + offset).astype(jnp.bfloat16)


def head_norm(values, gain_row):
    mean_square = jnp.mean(values * values, axis=-1, keepdims=True)
    return (values * lax.rsqrt(mean_square + EPS_NORM) * gain_row).astype(jnp.bfloat16)


def sigma_of(step_now):
    remain = 1.0 - step_now.astype(jnp.float32) / STEPS
    return 3.0 * remain / (1.0 + 2.0 * remain)


def per_device(
    hidden_img,
    hidden_txt,
    text_len,
    step_index,
    latent,
    cond,
    mod_weight,
    qkv_weight,
    kv_text_weight,
    q_gain,
    k_gain,
    out_weight,
    final_weight,
):
    row_pos = lax.axis_index("row")
    request = row_pos // 2
    lower_half = row_pos % 2 == 0
    img_rows, width_part = hidden_img.shape
    txt_rows = hidden_txt.shape[0]
    head_dim = q_gain.shape[0]
    qkv_cols = qkv_weight.shape[2]
    heads_here = qkv_cols // head_dim
    activated = jax.nn.silu(cond).astype(jnp.bfloat16)
    mod_local = mod_weight.reshape(mod_weight.shape[0], 7 * width_part)
    mod_terms = jnp.dot(activated, mod_local, preferred_element_type=jnp.float32).reshape(
        activated.shape[0], 7, width_part
    )
    mod_all = lax.psum(mod_terms, "row")
    mod_own = lax.dynamic_index_in_dim(mod_all, request, 0, keepdims=False)
    mod_full = lax.all_gather(mod_own, "col", axis=1, tiled=True)
    img_full, txt_full = (
        lax.all_gather(hidden_img, "col", axis=1, tiled=True),
        lax.all_gather(hidden_txt, "col", axis=1, tiled=True),
    )
    img_ready = modulate_full(img_full.astype(jnp.float32), mod_full[0], mod_full[1])
    txt_ready = modulate_full(txt_full.astype(jnp.float32), mod_full[3], mod_full[4])
    qkv_flat = qkv_weight.reshape(qkv_weight.shape[0], 3 * qkv_cols)
    kv_flat = kv_text_weight.reshape(kv_text_weight.shape[0], 2 * qkv_cols)
    img_proj = jnp.dot(
        img_ready,
        lax.all_gather(qkv_flat, "row", axis=0, tiled=True),
        preferred_element_type=jnp.float32,
    )
    txt_proj = jnp.dot(
        txt_ready,
        lax.all_gather(kv_flat, "row", axis=0, tiled=True),
        preferred_element_type=jnp.float32,
    )
    img_proj = img_proj.reshape(img_rows, 3, heads_here, head_dim)
    txt_proj = txt_proj.reshape(txt_rows, 2, heads_here, head_dim)
    queries = head_norm(img_proj[:, 0], q_gain)
    img_keys = head_norm(img_proj[:, 1], k_gain[0])
    img_values = img_proj[:, 2].astype(jnp.bfloat16)
    txt_keys = head_norm(txt_proj[:, 0], k_gain[1])
    txt_values = txt_proj[:, 1].astype(jnp.bfloat16)
    length = lax.dynamic_index_in_dim(text_len, request, 0, keepdims=False)
    scaling = head_dim ** (-0.5)
    partner = partner_2((img_keys, img_values, txt_keys, txt_values), "row", 0)

    def ordered(own_part, peer_part):
        return jnp.concatenate(
            [
                jnp.where(lower_half, own_part, peer_part),
                jnp.where(lower_half, peer_part, own_part),
            ],
            axis=0,
        )

    all_keys = jnp.concatenate(
        [ordered(img_keys, partner[0]), ordered(txt_keys, partner[2])], axis=0
    )
    all_values = jnp.concatenate(
        [ordered(img_values, partner[1]), ordered(txt_values, partner[3])], axis=0
    )
    key_valid = jnp.concatenate(
        [jnp.ones((2 * img_rows,), dtype=bool), jnp.arange(2 * txt_rows) < length]
    )

    def attend(head_ops):
        q_head, k_head, v_head = head_ops
        scores = jnp.dot(q_head, k_head.T, preferred_element_type=jnp.float32) * scaling
        scores = jnp.where(key_valid[None, :], scores, -jnp.inf)
        row_max = jnp.max(scores, axis=1, keepdims=True)
        weights = jnp.exp(scores - row_max)
        probabilities = (weights / jnp.sum(weights, axis=1, keepdims=True)).astype(jnp.bfloat16)
        return jnp.dot(probabilities, v_head, preferred_element_type=jnp.float32).astype(
            jnp.bfloat16
        )

    attended = lax.map(
        attend,
        (jnp.moveaxis(queries, 1, 0), jnp.moveaxis(all_keys, 1, 0), jnp.moveaxis(all_values, 1, 0)),
    )
    attended = jnp.moveaxis(attended, 0, 1).reshape(img_rows, qkv_cols)
    full_heads = lax.all_gather(attended, "col", axis=1, tiled=True)
    projected = jnp.dot(
        full_heads,
        lax.all_gather(out_weight, "row", axis=0, tiled=True),
        preferred_element_type=jnp.float32,
    )
    updated = (hidden_img.astype(jnp.float32) + mod_own[2] * projected).astype(jnp.bfloat16)
    head_full = lax.all_gather(final_weight, "row", axis=0, tiled=True)
    residual = lax.all_gather(updated, "col", axis=1, tiled=True)
    head_in = modulate_full(residual.astype(jnp.float32), mod_full[5], mod_full[6])
    velocity = jnp.dot(head_in, head_full, preferred_element_type=jnp.float32)
    step_now = lax.dynamic_index_in_dim(step_index, request, 0, keepdims=False)
    sigma_step = sigma_of(step_now + 1) - sigma_of(step_now)
    latent_next = latent + sigma_step * velocity
    return (velocity, latent_next)


def solution(mesh):
    in_specs = (
        P("row", "col"),
        P("row", "col"),
        P(),
        P(),
        P("row", None),
        P(None, "row"),
        P("row", None, "col"),
        P("row", None, "col"),
        P("row", None, "col"),
        P(),
        P(),
        P("row", "col"),
        P("row", None),
    )
    out_specs = (P("row", None), P("row", None))
    return jax.shard_map(
        per_device, mesh=mesh, in_specs=in_specs, out_specs=out_specs, check_vma=False
    )
```

profile of v0, /device:TPU:1, one launch (start us, length us, event | category | flops | bytes accessed | tf_op | source)
XLA Modules:
  0.0 753.6 jit_solution(9680876865259763626)
XLA Ops:
  8.1 1.6 fusion.48
  9.8 1.4 reshape.166
  15.4 61.1 %all_gather.30 = bf16[96,2432]{0,1:T(8,128)(2,1)S(1)} all-gather(bf16[96,152]{0,1:T(8,128)(2,1)} %param.16), channel_id=1, replica_groups=mesh['row'=32,'col'=16] {'col'}, dimensions={1}, use_global_device_ids=true | all-gather | bytes 496128 | tf_op jit(solution)/shard_map/all_gather | solution.py:70
  78.1 199.8 %all-reduce.3.cloned.1.call-done = f32[16,7,152]{2,0,1:T(8,128)} async-done(((f32[16,7,152]{2,0,1:T(8,128)}), f32[16,7,152]{2,0,1:T(8,128)}) %all-reduce.3.cloned.1.call-update) | async-done | bytes 68112 | tf_op jit(solution)/shard_map/psum | solution.py:65
  278.8 77.3 %all-gather = f32[1,7,2432]{1,0,2:T(1,128)S(1)} all-gather(f32[1,7,152]{1,0,2:T(1,128)S(1)} %copy.52), channel_id=2, replica_groups=mesh['row'=32,'col'=16] {'col'}, dimensions={2}, use_global_device_ids=true | all-gather | bytes 72352 | tf_op jit(solution)/shard_map/all_gather | solution.py:67
  356.1 42.9 %fusion.39 = (f32[2432]{0:T(1024)}, f32[2432]{0:T(1024)S(1)}, f32[2432]{0:T(1024)S(1)}, f32[2432]{0:T(1024)}, f32[2432]{0:T(1024)}, /*index=5*/f32[2432]{0:T(1024)}) fusion(f32[1,7,2432]{1,0,2:T(1,128)S(1)} %all-gather), kind=kLoop, calls=%fused_computation.55 | loop fusion | flops 7296 | bytes 116736 | tf_op jit(solution)/shard_map/add | solution.py:24
  399.0 2.2 reshape.167
  402.4 6.7 collective-permute-start.3
  409.2 1.9 collective-permute-start.1
  413.1 14.4 %all-gather.16.cloned.1.call-done = bf16[32,76,384]{2,1,0:T(8,128)(2,1)} async-done(((bf16[1,76,384]{2,1,0:T(8,128)(2,1)}), bf16[32,76,384]{2,1,0:T(8,128)(2,1)}) %all-gather.16.cloned.1.call-update) | async-done | bytes 1867792 | tf_op jit(solution)/shard_map/all_gather | solution.py:78
  427.5 2.5 reshape.165
  429.9 103.8 %all-gather.10.cloned.1.call-done = bf16[512,2432]{0,1:T(8,128)(2,1)} async-done(((bf16[512,152]{0,1:T(8,128)(2,1)}), bf16[512,2432]{0,1:T(8,128)(2,1)}) %all-gather.10.cloned.1.call-update) | async-done | bytes 2490384 | tf_op jit(solution)/shard_map/all_gather | solution.py:69
  533.7 2.6 convert_reduce_fusion.1
  536.4 1.9 fusion.24
  538.5 2.8 collective-permute-start
  541.3 2.1 collective-permute-start.2
  544.9 3.1 while.10
  548.7 44.3 %all_gather.33 = bf16[2048,152]{1,0:T(8,128)(2,1)S(1)} all-gather(bf16[64,152]{1,0:T(8,128)(2,1)S(1)} %copy-done.6), channel_id=1, replica_groups=mesh['row'=32,'col'=16] {'row'}, dimensions={0}, use_global_device_ids=true | all-gather | bytes 642048 | tf_op jit(solution)/shard_map/all_gather | solution.py:135
  593.8 45.6 %all-gather.12.cloned.1.call-done = bf16[512,2048]{0,1:T(8,128)(2,1)} async-done(((bf16[512,128]{0,1:T(8,128)(2,1)}), bf16[512,2048]{0,1:T(8,128)(2,1)}) %all-gather.12.cloned.1.call-update) | async-done | bytes 2097168 | tf_op jit(solution)/shard_map/all_gather | solution.py:132
  639.4 2.8 fusion.41
  644.2 45.2 %all-gather.3 = bf16[32,76,64]{1,2,0:T(8,128)(2,1)S(1)} all-gather(bf16[1,76,64]{1,2,0:T(8,128)(2,1)S(1)} %bitcast.104), channel_id=1, replica_groups=mesh['row'=32,'col'=16] {'row'}, dimensions={0}, use_global_device_ids=true | all-gather | bytes 321024 | tf_op jit(solution)/shard_map/all_gather | solution.py:139
  690.6 51.6 %all-gather.14.cloned.1.call-done = bf16[512,2432]{0,1:T(8,128)(2,1)} async-done(((bf16[512,152]{0,1:T(8,128)(2,1)}), bf16[512,2432]{0,1:T(8,128)(2,1)}) %all-gather.14.cloned.1.call-update) | async-done | bytes 2490384 | tf_op jit(solution)/shard_map/all_gather | solution.py:140
  742.3 2.6 convert_reduce_fusion
  744.9 1.8 multiply_add_fusion
  (87 shorter events, 18.7 us)
Async XLA Ops:
  7.2 270.7 %all-reduce.3.cloned.1.call-start = ((), (), s32[]{:S(2)}) async-start(), calls=%async_computation | async-start | bytes 229376 | tf_op jit(solution)/shard_map/psum | solution.py:65
  9.8 389.2 %all-gather.18.cloned.1.call-start = ((), (), s32[]{:S(2)}) async-start(), calls=%async_computation.5 | async-start | bytes 1351680 | tf_op jit(solution)/shard_map/all_gather | solution.py:83
  11.3 416.2 %all-gather.16.cloned.1.call-start = ((), (), s32[]{:S(2)}) async-start(), calls=%async_computation.4 | async-start | bytes 2027520 | tf_op jit(solution)/shard_map/all_gather | solution.py:78
  12.9 520.9 %all-gather.10.cloned.1.call-start = ((), (), s32[]{:S(2)}) async-start(), calls=%async_computation.1 | async-start | bytes 2646016 | tf_op jit(solution)/shard_map/all_gather | solution.py:69
  13.5 626.0 %all-gather.12.cloned.1.call-start = ((), (), s32[]{:S(2)}) async-start(), calls=%async_computation.2 | async-start | bytes 2228224 | tf_op jit(solution)/shard_map/all_gather | solution.py:132
  402.4 8.8 %collective-permute-start.3 = (bf16[96,2,64]{0,2,1:T(8,128)(2,1)S(1)}, bf16[96,2,64]{0,2,1:T(8,128)(2,1)S(1)}, u32[]{:S(2)}, u32[]{:S(2)}) collective-permute-start(bf16[96,2,64]{0,2,1:T(8,128)(2,1)S(1)} %fusion.52), channel_id=1, source_target_pairs={{0,16},{16,0},{32,48},{48,32},{64,80},{80,64},{96,112},{112,96},{1... | collective-permute-start | bytes 73736 | tf_op jit(solution)/shard_map/ppermute | solution.py:17
  409.2 3.1 collective-permute-start.1
  413.1 123.3 %copy-start.10 = (f32[2432]{0:T(1024)S(1)}, f32[2432]{0:T(1024)}, u32[]{:S(2)}) copy-start(f32[2432]{0:T(1024)} %get-tuple-element.48) | copy-start | bytes 29188
  413.1 123.3 %copy-start.11 = (f32[2432]{0:T(1024)S(1)}, f32[2432]{0:T(1024)}, u32[]{:S(2)}) copy-start(f32[2432]{0:T(1024)} %get-tuple-element.49) | copy-start | bytes 29188
  533.7 2.6 copy-start.1
  536.3 2.0 copy-start.12
  536.3 2.0 copy-start.13
  538.2 6.5 copy-start.5
  538.5 5.0 collective-permute-start
  541.3 3.4 collective-permute-start.2
  544.9 3.8 copy-start.6
  544.9 94.5 %copy-start.3 = (bf16[512,152]{0,1:T(8,128)(2,1)S(1)}, bf16[512,152]{0,1:T(8,128)(2,1)}, u32[]{:S(2)}) copy-start(bf16[512,152]{0,1:T(8,128)(2,1)} %param.15) | copy-start | bytes 466948
  548.0 94.3 %copy-start.15 = (s32[16]{0:T(128)S(1)}, s32[16]{0:T(128)}, u32[]{:S(2)}) copy-start(s32[16]{0:T(128)} %param.18) | copy-start | bytes 196
  548.0 96.2 %copy-start.7 = (bf16[76,64]{0,1:T(8,128)(2,1)S(1)}, bf16[76,64]{0,1:T(8,128)(2,1)}, u32[]{:S(2)}) copy-start(bf16[76,64]{0,1:T(8,128)(2,1)} %param.27) | copy-start | bytes 29188
  548.7 193.6 %all-gather.14.cloned.1.call-start = ((), (), s32[]{:S(2)}) async-start(), calls=%async_computation.3 | async-start | bytes 2646016 | tf_op jit(solution)/shard_map/all_gather | solution.py:140
  642.3 102.6 %copy-start.8 = (f32[2432]{0:T(1024)S(1)}, f32[2432]{0:T(1024)}, u32[]{:S(2)}) copy-start(f32[2432]{0:T(1024)} %get-tuple-element.45) | copy-start | bytes 29188
  642.3 102.6 %copy-start.9 = (f32[2432]{0:T(1024)S(1)}, f32[2432]{0:T(1024)}, u32[]{:S(2)}) copy-start(f32[2432]{0:T(1024)} %get-tuple-element.50) | copy-start | bytes 29188
  642.3 102.6 %copy-start.14 = (f32[512,64]{0,1:T(8,128)S(1)}, f32[512,64]{0,1:T(8,128)}, u32[]{:S(2)}) copy-start(f32[512,64]{0,1:T(8,128)} %param.19) | copy-start | bytes 393220
  742.3 2.6 copy-start.2
  (2 other events, 1.6 us)
Sparse Core Ops, SparseCore 0:
  11.5 266.3 all-reduce.2
  280.2 76.0 all-gather.17
  359.3 68.1 all-gather.15
  430.8 102.8 all-gather.9
  548.8 90.5 all-gather.11
  642.8 99.4 all-gather.13
where the time goes:
time: 754 us
  waiting for transfers between devices  417 us (55%)
  blocking collectives  228 us (30%)
  other arithmetic  51.4 us (7%)
  local copies, waits for them, and re-layouts  16 us (2%)
  between operations  15.9 us (2%)
  starting transfers between devices  13.8 us (2%)
  matrix products  11.6 us (2%)
    psum x1, waiting for transfers between devices, per_device(): mod_all = lax.psum(mod_terms, 'row')  200 us
    all_gather x1, waiting for transfers between devices, per_device(): lax.all_gather(hidden_img, 'col', axis=1, tiled=True)  104 us
    all_gather x1, blocking collectives, per_device(): mod_full = lax.all_gather(mod_own, 'col', axis=1, tiled=True)  77.3 us
    all_gather x1, blocking collectives, per_device(): lax.all_gather(hidden_txt, 'col', axis=1, tiled=True)  61.1 us
    all_gather x1, waiting for transfers between devices, per_device(): residual = lax.all_gather(updated, 'col', axis=1, tiled=True)  51.6 us
    all_gather x1, waiting for transfers between devices, per_device(): full_heads = lax.all_gather(attended, 'col', axis=1, tiled=True)  45.6 us
    all_gather x1, blocking collectives, per_device(): head_full = lax.all_gather(final_weight, 'row', axis=0, tiled=True)  45.2 us
    all_gather x1, blocking collectives, per_device(): lax.all_gather(out_weight, 'row', axis=0, tiled=True)  44.3 us
  transfers between devices with their start and end apart: 10, of which 7 were waited for; matrix products, arithmetic and copies ran while one was open for 8% of the time, Pallas kernels for 0%

commit v1 on v0

--- a/solution.py
+++ b/solution.py
@@ -65,8 +65,11 @@
     mod_all = lax.psum(mod_terms, "row")
     mod_own = lax.dynamic_index_in_dim(mod_all, request, 0, keepdims=False)
     mod_full = lax.all_gather(mod_own, "col", axis=1, tiled=True)
+    read_pages = lambda patch, along_dim: jnp.concatenate(
+        lax.all_to_all(jnp.stack([patch] * lax.axis_size("col")), "col", 0, 0), axis=along_dim
+    )
     img_full, txt_full = (
-        lax.all_gather(hidden_img, "col", axis=1, tiled=True),
+        read_pages(hidden_img, 1),
         lax.all_gather(hidden_txt, "col", axis=1, tiled=True),
     )
     img_ready = modulate_full(img_full.astype(jnp.float32), mod_full[0], mod_full[1])

time: 754 us -> 718 us (0.952)
  waiting for transfers between devices: 417 us -> 268 us
  blocking collectives: 228 us -> 322 us
  starting transfers between devices: 13.8 us -> 31.9 us
    all_gather x1 -> x0, waiting for transfers between devices: 104 us -> none  [per_device(): lax.all_gather(hidden_img, 'col', axis=1, tiled=True)]
    all_gather x1, blocking collectives: 61.1 us -> 151 us  [per_device(): lax.all_gather(hidden_txt, 'col', axis=1, tiled=True)]
    psum x1, waiting for transfers between devices: 200 us -> 156 us  [per_device(): mod_all = lax.psum(mod_terms, 'row')]
    all_to_all x0 -> x1, starting transfers between devices: none -> 18.5 us  [per_device(): lax.all_to_all(jnp.stack([patch] * lax.axis_size('col')), 'col', 0, 0)]
  transfers between devices with their start and end apart: 10 -> 10, of which waited for: 7 -> 6; matrix products, arithmetic and copies ran while one was open for 8% -> 9% of each run, Pallas kernels for 0% -> 0%
where the time goes in v1:
time: 718 us
  blocking collectives  322 us (45%)
  waiting for transfers between devices  268 us (37%)
  other arithmetic  49.1 us (7%)
  starting transfers between devices  31.9 us (4%)
  local copies, waits for them, and re-layouts  20.1 us (3%)
  between operations  15.7 us (2%)
  matrix products  11.5 us (2%)
    psum x1, waiting for transfers between devices, per_device(): mod_all = lax.psum(mod_terms, 'row')  156 us
    all_gather x1, blocking collectives, per_device(): lax.all_gather(hidden_txt, 'col', axis=1, tiled=True)  151 us
    all_gather x1, blocking collectives, per_device(): mod_full = lax.all_gather(mod_own, 'col', axis=1, tiled=True)  77.3 us
    all_gather x1, waiting for transfers between devices, per_device(): residual = lax.all_gather(updated, 'col', axis=1, tiled=True)  51.2 us
    all_gather x1, blocking collectives, per_device(): lax.all_gather(out_weight, 'row', axis=0, tiled=True)  47.4 us
    all_gather x1, waiting for transfers between devices, per_device(): full_heads = lax.all_gather(attended, 'col', axis=1, tiled=True)  46 us
    all_gather x1, blocking collectives, per_device(): head_full = lax.all_gather(final_weight, 'row', axis=0, tiled=True)  45.9 us
    add x1, other arithmetic, modulate_full(): return (normed * (1.0 + stretch) + offset).astype(jnp.bfloat16)  42.5 us
  transfers between devices with their start and end apart: 10, of which 6 were waited for; matrix products, arithmetic and copies ran while one was open for 9% of the time, Pallas kernels for 0%

profile of v1, /device:TPU:1, one launch (start us, length us, event | category | flops | bytes accessed | tf_op | source)
XLA Modules:
  0.0 717.7 jit_solution(12694141570608553148)
XLA Ops:
  7.2 2.6 stack.2
  9.8 18.5 %all-to-all-start = ((bf16[16,512,152]{1,2,0:T(8,128)(2,1)}), bf16[16,512,152]{1,2,0:T(8,128)(2,1)S(1)}, u32[]{:S(2)}, u32[]{:S(2)}) async-start(bf16[16,512,152]{1,2,0:T(8,128)(2,1)} %stack.2), calls=%async_computation | async-start | bytes 4980736 | tf_op jit(solution)/shard_map/all_to_all | solution.py:69
  32.4 151.0 %all_gather.26 = bf16[96,2432]{0,1:T(8,128)(2,1)S(1)} all-gather(bf16[96,152]{0,1:T(8,128)(2,1)S(1)} %copy-done.7), channel_id=1, replica_groups=mesh['row'=32,'col'=16] {'col'}, dimensions={1}, use_global_device_ids=true | all-gather | bytes 496128 | tf_op jit(solution)/shard_map/all_gather | solution.py:73
  183.7 156.1 %all-reduce.3.cloned.1.call-done = f32[16,7,152]{2,0,1:T(8,128)} async-done(((f32[16,7,152]{2,0,1:T(8,128)}), f32[16,7,152]{2,0,1:T(8,128)}) %all-reduce.3.cloned.1.call-update) | async-done | bytes 68112 | tf_op jit(solution)/shard_map/psum | solution.py:65
  340.7 77.3 %all-gather = f32[1,7,2432]{1,0,2:T(1,128)S(1)} all-gather(f32[1,7,152]{1,0,2:T(1,128)S(1)} %copy.37), channel_id=2, replica_groups=mesh['row'=32,'col'=16] {'col'}, dimensions={2}, use_global_device_ids=true | all-gather | bytes 72352 | tf_op jit(solution)/shard_map/all_gather | solution.py:67
  418.0 42.5 %fusion.33 = (f32[2432]{0:T(1024)S(1)}, f32[2432]{0:T(1024)S(1)}, f32[2432]{0:T(1024)S(1)}, f32[2432]{0:T(1024)S(1)}, f32[2432]{0:T(1024)S(1)}, /*index=5*/f32[2432]{0:T(1024)S(1)}) fusion(f32[1,7,2432]{1,0,2:T(1,128)S(1)} %all-gather), kind=kLoop, calls=%fused_computation.50 | loop fusion | flops 7296 | bytes 116736 | tf_op jit(solution)/shard_map/add | solution.py:24
  460.7 2.9 reshape.190
  463.7 2.5 fusion.36
  466.3 6.7 collective-permute-start.3
  473.1 2.1 collective-permute-start.1
  476.3 12.6 %all-gather.13.cloned.1.call-done = bf16[32,76,384]{2,1,0:T(8,128)(2,1)} async-done(((bf16[1,76,384]{2,1,0:T(8,128)(2,1)}), bf16[32,76,384]{2,1,0:T(8,128)(2,1)}) %all-gather.13.cloned.1.call-update) | async-done | bytes 1867792 | tf_op jit(solution)/shard_map/all_gather | solution.py:81
  488.9 3.7 reshape.188
  492.6 3.9 copy.39
  498.7 1.2 fusion.50
  500.0 2.2 collective-permute-start.2
  502.3 2.1 collective-permute-start
  505.7 3.1 while.10
  509.6 47.4 %all_gather.29 = bf16[2048,152]{1,0:T(8,128)(2,1)S(1)} all-gather(bf16[64,152]{1,0:T(8,128)(2,1)S(1)} %copy-done.9), channel_id=1, replica_groups=mesh['row'=32,'col'=16] {'row'}, dimensions={0}, use_global_device_ids=true | all-gather | bytes 642048 | tf_op jit(solution)/shard_map/all_gather | solution.py:138
  557.7 46.0 %all-gather.9.cloned.1.call-done = bf16[512,2048]{0,1:T(8,128)(2,1)} async-done(((bf16[512,128]{0,1:T(8,128)(2,1)}), bf16[512,2048]{0,1:T(8,128)(2,1)}) %all-gather.9.cloned.1.call-update) | async-done | bytes 2097168 | tf_op jit(solution)/shard_map/all_gather | solution.py:135
  603.7 2.8 fusion.35
  608.5 45.9 %all-gather.3 = bf16[32,76,64]{1,2,0:T(8,128)(2,1)S(1)} all-gather(bf16[1,76,64]{1,2,0:T(8,128)(2,1)S(1)} %bitcast.110), channel_id=1, replica_groups=mesh['row'=32,'col'=16] {'row'}, dimensions={0}, use_global_device_ids=true | all-gather | bytes 321024 | tf_op jit(solution)/shard_map/all_gather | solution.py:142
  655.6 51.2 %all-gather.11.cloned.1.call-done = bf16[512,2432]{0,1:T(8,128)(2,1)} async-done(((bf16[512,152]{0,1:T(8,128)(2,1)}), bf16[512,2432]{0,1:T(8,128)(2,1)}) %all-gather.11.cloned.1.call-update) | async-done | bytes 2490384 | tf_op jit(solution)/shard_map/all_gather | solution.py:143
  706.8 2.6 convert_reduce_fusion
  709.4 1.8 multiply_add_fusion
  (93 shorter events, 16.4 us)
Async XLA Ops:
  7.2 21.2 %copy-start = (bf16[76,7,152]{0,2,1:T(8,128)(2,1)S(1)}, bf16[76,7,152]{0,2,1:T(8,128)(2,1)}, u32[]{:S(2)}) copy-start(bf16[76,7,152]{0,2,1:T(8,128)(2,1)} %param.21) | copy-start | bytes 485188
  9.7 18.6 %copy-start.11 = (f32[16,76]{1,0:T(8,128)S(1)}, f32[16,76]{1,0:T(8,128)}, u32[]{:S(2)}) copy-start(f32[16,76]{1,0:T(8,128)} %param.20) | copy-start | bytes 14596
  9.7 19.6 %copy-start.8 = (bf16[76,2,128]{2,1,0:T(2,128)(2,1)S(1)}, bf16[76,2,128]{2,1,0:T(2,128)(2,1)}, u32[]{:S(2)}) copy-start(bf16[76,2,128]{2,1,0:T(2,128)(2,1)} %param.23) | copy-start | bytes 116740
  9.7 20.4 %copy-start.6 = (bf16[76,3,128]{2,0,1:T(8,128)(2,1)S(1)}, bf16[76,3,128]{2,0,1:T(8,128)(2,1)}, u32[]{:S(2)}) copy-start(bf16[76,3,128]{2,0,1:T(8,128)(2,1)} %param.22) | copy-start | bytes 175108
  9.7 21.2 %copy-start.15 = (s32[16]{0:T(128)S(1)}, s32[16]{0:T(128)}, u32[]{:S(2)}) copy-start(s32[16]{0:T(128)} %param.17) | copy-start | bytes 196
  9.8 22.6 %copy-start.7 = (bf16[96,152]{0,1:T(8,128)(2,1)S(1)}, bf16[96,152]{0,1:T(8,128)(2,1)}, u32[]{:S(2)}) copy-start(bf16[96,152]{0,1:T(8,128)(2,1)} %param.16) | copy-start | bytes 87556
  9.8 173.9 %copy-start.12 = (f32[2,64]{1,0:T(2,128)S(1)}, f32[2,64]{1,0:T(2,128)}, u32[]{:S(2)}) copy-start(f32[2,64]{1,0:T(2,128)} %param.25) | copy-start | bytes 1540
  9.8 486.7 %all-to-all-start = ((bf16[16,512,152]{1,2,0:T(8,128)(2,1)}), bf16[16,512,152]{1,2,0:T(8,128)(2,1)S(1)}, u32[]{:S(2)}, u32[]{:S(2)}) async-start(bf16[16,512,152]{1,2,0:T(8,128)(2,1)} %stack.2), calls=%async_computation | async-start | bytes 4980736 | tf_op jit(solution)/shard_map/all_to_all | solution.py:69
  28.3 311.5 %all-reduce.3.cloned.1.call-start = ((), (), s32[]{:S(2)}) async-start(), calls=%async_computation.1 | async-start | bytes 229376 | tf_op jit(solution)/shard_map/psum | solution.py:65
  29.3 431.4 %all-gather.15.cloned.1.call-start = ((), (), s32[]{:S(2)}) async-start(), calls=%async_computation.5 | async-start | bytes 1351680 | tf_op jit(solution)/shard_map/all_gather | solution.py:86
  30.1 458.8 %all-gather.13.cloned.1.call-start = ((), (), s32[]{:S(2)}) async-start(), calls=%async_computation.4 | async-start | bytes 2027520 | tf_op jit(solution)/shard_map/all_gather | solution.py:81
  30.9 572.8 %all-gather.9.cloned.1.call-start = ((), (), s32[]{:S(2)}) async-start(), calls=%async_computation.2 | async-start | bytes 2228224 | tf_op jit(solution)/shard_map/all_gather | solution.py:135
  466.3 8.9 %collective-permute-start.3 = (bf16[96,2,64]{0,2,1:T(8,128)(2,1)S(1)}, bf16[96,2,64]{0,2,1:T(8,128)(2,1)S(1)}, u32[]{:S(2)}, u32[]{:S(2)}) collective-permute-start(bf16[96,2,64]{0,2,1:T(8,128)(2,1)S(1)} %fusion.46), channel_id=1, source_target_pairs={{0,16},{16,0},{32,48},{48,32},{64,80},{80,64},{96,112},{112,96},{1... | collective-permute-start | bytes 73736 | tf_op jit(solution)/shard_map/ppermute | solution.py:17
  473.1 3.1 collective-permute-start.1
  498.7 3.5 copy-start.13
  499.9 5.8 copy-start.4
  500.0 4.5 collective-permute-start.2
  502.3 3.2 collective-permute-start
  505.7 3.8 copy-start.9
  505.7 98.0 %copy-start.3 = (bf16[512,152]{0,1:T(8,128)(2,1)S(1)}, bf16[512,152]{0,1:T(8,128)(2,1)}, u32[]{:S(2)}) copy-start(bf16[512,152]{0,1:T(8,128)(2,1)} %param.15) | copy-start | bytes 466948
  508.8 97.7 %copy-start.16 = (s32[16]{0:T(128)S(1)}, s32[16]{0:T(128)}, u32[]{:S(2)}) copy-start(s32[16]{0:T(128)} %param.18) | copy-start | bytes 196
  508.9 99.6 %copy-start.10 = (bf16[76,64]{0,1:T(8,128)(2,1)S(1)}, bf16[76,64]{0,1:T(8,128)(2,1)}, u32[]{:S(2)}) copy-start(bf16[76,64]{0,1:T(8,128)(2,1)} %param.27) | copy-start | bytes 29188
  509.5 197.3 %all-gather.11.cloned.1.call-start = ((), (), s32[]{:S(2)}) async-start(), calls=%async_computation.3 | async-start | bytes 2646016 | tf_op jit(solution)/shard_map/all_gather | solution.py:143
  606.5 102.8 %copy-start.14 = (f32[512,64]{0,1:T(8,128)S(1)}, f32[512,64]{0,1:T(8,128)}, u32[]{:S(2)}) copy-start(f32[512,64]{0,1:T(8,128)} %param.19) | copy-start | bytes 393220
  (3 other events, 4.8 us)
Sparse Core Ops, SparseCore 0:
  32.6 307.1 all-reduce.2
  342.2 76.0 all-gather.14
  420.6 68.2 all-gather.12
  509.6 94.0 all-gather.8
  607.0 99.7 all-gather.10
